TPU v7x, 32 devices: a whole 2x2x4 slice. The times are simulated.
32 devices in a mesh: col: 8 (over z, y), lev: 4 (over x, core).
Axes of the slice: x: 2, y: 2, z: 4, core: 2. Of those that a mesh axis runs over, the one named last changes fastest.
Arguments:
- state_anom: bfloat16 [48, 64, 8192], P('lev', None, 'col'), may hold values from -6 to 6
- error_sum: float32 [48, 8192], P('lev', 'col'), may hold values from -3 to 3
- obs_anom: bfloat16 [64, 16384], P('lev', 'col'), may hold values from -6 to 6
- local_weight: float32 [32, 16384], P(None, 'col'), may hold values from 0.05 to 1
- neighbours: int32 [32, 16384], P(None, 'col'), may hold values from 0 to 3071, as said below
- innovation: float32 [16384], P(('col', 'lev')), may hold values from -6 to 6
- obs_type: int32 [16384], P(('col', 'lev')), may hold values from 0 to 31
- live: int32 [16384], P(('col', 'lev')), may hold values 0 or 1
Outputs:
- impact: float32 [16384], P(('col', 'lev'))
- type_impact: float32 [32], replicated
Inputs may be any that keep to these rules, and one draw needn't show every extreme that they name: Observation o lies in column tile o // 2048; the column (o // 2048 - 1) * 1024 + neighbours[n, o] lies in that tile or the tile on either side of it, inside the grid.
All inputs are finite; a program needn't handle non-finite values. No bound on the sum of `live` on one device may be relied on, other than what follows from the above.
Results may differ from a plain program's by a relative error of at most 0.0003.
Values may be sent and summed in bfloat16 or wider, within the bound.
A program may use at most 64 MiB of HBM per device.

v0:
```python
import math

import jax
import jax.numpy as jnp
from jax import lax
from jax.sharding import PartitionSpec as P

MEMBERS = 64
NTYPE = 32


def with_halo(cells, sides, width):
    for axis, dim in sides:
        count = lax.axis_size(axis)
        ends = count - 1
        head = lax.slice_in_dim(cells, 0, width, axis=dim)
        tail = lax.slice_in_dim(cells, cells.shape[dim] - width, cells.shape[dim], axis=dim)
        cells = jnp.concatenate(
            [
                lax.ppermute(tail, axis, [(i, (i + 1) % count) for i in range(ends)]),
                cells,
                lax.ppermute(head, axis, [((i + 1) % count, i) for i in range(ends)]),
            ],
            axis=dim,
        )
    return cells


def block_pairs(extended, anom, weight, index):
    span = extended.shape[1]
    column_ids = lax.broadcasted_iota(jnp.int32, (span, index.shape[1]), 0)
    table = jnp.sum(
        jnp.where(index[:, None, :] == column_ids[None, :, :], weight[:, None, :], 0.0), axis=0
    )
    spread = jnp.dot(
        extended, table, precision=lax.Precision.HIGHEST, preferred_element_type=jnp.float32
    )
    return jnp.sum(anom.astype(jnp.float32) * spread, axis=0)


def shards(state_anom, error_sum, obs_anom, local_weight, neighbours, innovation, obs_type, live):
    columns = state_anom.shape[2]
    regrouped = lax.all_to_all(state_anom, "lev", split_axis=1, concat_axis=0, tiled=True)
    all_error = lax.all_gather(error_sum, "lev", axis=0, tiled=True)
    sens = jnp.einsum(
        "lkc,lc->kc", regrouped.astype(jnp.float32), all_error, precision=lax.Precision.HIGHEST
    )
    extended = with_halo(sens, (("col", 1),), columns)
    obs_slots = obs_anom.shape[1]
    step_rows = math.gcd(obs_slots, 512)
    count = obs_slots // step_rows
    groups = obs_anom.shape[0]
    anom_blocks = jnp.transpose(obs_anom.reshape(groups, count, step_rows), (1, 0, 2))
    weight_blocks = jnp.transpose(
        local_weight.reshape(local_weight.shape[0], count, step_rows), (1, 0, 2)
    )
    index_blocks = jnp.transpose(
        neighbours.reshape(neighbours.shape[0], count, step_rows), (1, 0, 2)
    )

    def one_block(items):
        return block_pairs(extended, items[0], items[1], items[2])

    partial_pair = lax.map(one_block, (anom_blocks, weight_blocks, index_blocks)).reshape(obs_slots)
    pair = lax.psum_scatter(partial_pair, "lev", scatter_dimension=0, tiled=True)
    impact = pair * innovation * live.astype(jnp.float32) / (MEMBERS - 1.0)
    onehot = (obs_type[None, :] == jnp.arange(NTYPE, dtype=jnp.int32)[:, None]).astype(jnp.float32)
    type_part = jnp.sum(onehot * impact[None, :], axis=1)
    type_impact = lax.psum(type_part, ("col", "lev"))
    return (impact, type_impact)


def solution(mesh):
    in_specs = (
        P("lev", None, "col"),
        P("lev", "col"),
        P("lev", "col"),
        P(None, "col"),
        P(None, "col"),
        P(("col", "lev")),
        P(("col", "lev")),
        P(("col", "lev")),
    )
    out_specs = (P(("col", "lev")), P())
    return jax.shard_map(shards, mesh=mesh, in_specs=in_specs, out_specs=out_specs, check_vma=False)
```

profile of v0, /device:TPU:0, one launch (start us, length us, event | category | flops | bytes accessed | tf_op | source)
XLA Modules:
  0.0 241.2 jit_solution(3400720630463568245)
XLA Ops:
  0.6 3.7 %copy.23 = bf16[12,64,1024]{2,0,1:T(8,128)(2,1)} copy(bf16[12,64,1024]{2,1,0:T(8,128)(2,1)} %param.10) | data formatting | bytes 3145728 | tf_op args[0]
  4.4 4.4 %all-to-all-start = ((bf16[12,64,1024]{2,0,1:T(8,128)(2,1)}), bf16[12,64,1024]{2,0,1:T(8,128)(2,1)S(1)}, u32[]{:S(2)}, u32[]{:S(2)}) async-start(bf16[12,64,1024]{2,0,1:T(8,128)(2,1)} %copy.23), calls=%async_computation | async-start | bytes 4194304 | tf_op jit(solution)/shard_map/all_to_all | solution.py:43
  8.7 27.9 %all-gather = f32[4,12,1024]{2,1,0:T(8,128)S(1)} all-gather(f32[1,12,1024]{2,1,0:T(8,128)S(1)} %bitcast.60), channel_id=1, replica_groups=mesh['col'=8,'lev'=4] {'lev'}, dimensions={0}, use_global_device_ids=true | all-gather | bytes 245760 | tf_op jit(solution)/shard_map/all_gather | solution.py:44
  36.7 0.9 copy.36
  37.6 0.4 multiply_reduce_fusion
  38.0 4.2 %collective-permute-start = (f32[16,1024]{1,0:T(8,128)S(1)}, f32[16,1024]{1,0:T(8,128)S(1)}, u32[]{:S(2)}, u32[]{:S(2)}) collective-permute-start(f32[16,1024]{1,0:T(8,128)S(1)} %bitcast.55), channel_id=1, source_target_pairs={{0,4},{4,8},{8,12},{12,16},{16,20},{20,24},{24,28},{1,5},{5,9},{9,... | collective-permute-start | bytes 196616 | tf_op jit(solution)/shard_map/ppermute | solution.py:20
  42.3 1.3 collective-permute-start.1
  43.6 0.2 reshape.25
  43.8 0.2 reshape.26
  44.0 0.6 dynamic-slice
  45.3 3.1 %collective-permute-done.1 = f32[16,1024]{1,0:T(8,128)S(1)} collective-permute-done((f32[16,1024]{1,0:T(8,128)S(1)}, f32[16,1024]{1,0:T(8,128)S(1)}, u32[]{:S(2)}, u32[]{:S(2)}) %collective-permute-start.1) | collective-permute-done | bytes 65568 | tf_op jit(solution)/shard_map/ppermute | solution.py:22
  48.5 146.3 %while.10 = (s32[]{:T(128)}, f32[4,512]{1,0:T(4,128)S(1)}, bf16[4,16,512]{2,1,0:T(8,128)(2,1)S(1)}, s32[4,32,512]{2,0,1:T(4,128)S(1)}, f32[4,32,512]{2,0,1:T(4,1...) while((s32[]{:T(128)}, f32[4,512]{1,0:T(4,128)S(1)}, bf16[4,16,512]{2,1,0:T(8,128)(2,1)S(1)}, ...), condition=%wide.region_3.4_spmd, body=%wide.region_0.3_spmd.sunk | while | flops 451436032 | bytes 13457509 | solution.py:64
  48.5 0.1 constant_dynamic-slice_fusion.4
  48.6 0.1 constant_dynamic-slice_fusion.5
  48.6 30.9 %select_reduce_fusion.3 = f32[3072,512]{1,0:T(8,128)} fusion(f32[32,512]{1,0:T(8,128)S(1)} %bitcast.50, s32[32,512]{1,0:T(8,128)S(1)} %bitcast.51), kind=kLoop, calls=%fused_computation.clone.1 | loop fusion | flops 149422080 | bytes 6422528 | tf_op jit(solution)/shard_map/while/body/eval_jaxpr/reduce_sum | solution.py:32
  79.6 5.4 %fusion.11 = f32[512]{0:T(512)S(1)} fusion(f32[3072,512]{1,0:T(8,128)} %select_reduce_fusion.3, f32[16,3072]{1,0:T(8,128)S(1)} %get-tuple-element.129, bf16[4,16,512]{2,1,0:T(8,128)(2,1)S(1)} %get-tuple-element.126, s32[]{:T(128)} %get-tuple-element.116), kind=kOutput, calls=%fused_computation.4.clone.1 | convolution fusion | flops 302013952 | bytes 6506500 | tf_op jit(solution)/shard_map/while/body/eval_jaxpr/dot_general | solution.py:35
  85.0 0.1 constant_dynamic-slice_fusion.4
  85.1 0.1 constant_dynamic-slice_fusion.5
  85.2 30.9 %select_reduce_fusion.3 = f32[3072,512]{1,0:T(8,128)} fusion(f32[32,512]{1,0:T(8,128)S(1)} %bitcast.50, s32[32,512]{1,0:T(8,128)S(1)} %bitcast.51), kind=kLoop, calls=%fused_computation.clone.1 | loop fusion | flops 149422080 | bytes 6422528 | tf_op jit(solution)/shard_map/while/body/eval_jaxpr/reduce_sum | solution.py:32
  116.1 5.4 %fusion.11 = f32[512]{0:T(512)S(1)} fusion(f32[3072,512]{1,0:T(8,128)} %select_reduce_fusion.3, f32[16,3072]{1,0:T(8,128)S(1)} %get-tuple-element.129, bf16[4,16,512]{2,1,0:T(8,128)(2,1)S(1)} %get-tuple-element.126, s32[]{:T(128)} %get-tuple-element.116), kind=kOutput, calls=%fused_computation.4.clone.1 | convolution fusion | flops 302013952 | bytes 6506500 | tf_op jit(solution)/shard_map/while/body/eval_jaxpr/dot_general | solution.py:35
  121.6 0.1 constant_dynamic-slice_fusion.4
  121.7 0.1 constant_dynamic-slice_fusion.5
  121.8 30.9 %select_reduce_fusion.3 = f32[3072,512]{1,0:T(8,128)} fusion(f32[32,512]{1,0:T(8,128)S(1)} %bitcast.50, s32[32,512]{1,0:T(8,128)S(1)} %bitcast.51), kind=kLoop, calls=%fused_computation.clone.1 | loop fusion | flops 149422080 | bytes 6422528 | tf_op jit(solution)/shard_map/while/body/eval_jaxpr/reduce_sum | solution.py:32
  152.7 5.4 %fusion.11 = f32[512]{0:T(512)S(1)} fusion(f32[3072,512]{1,0:T(8,128)} %select_reduce_fusion.3, f32[16,3072]{1,0:T(8,128)S(1)} %get-tuple-element.129, bf16[4,16,512]{2,1,0:T(8,128)(2,1)S(1)} %get-tuple-element.126, s32[]{:T(128)} %get-tuple-element.116), kind=kOutput, calls=%fused_computation.4.clone.1 | convolution fusion | flops 302013952 | bytes 6506500 | tf_op jit(solution)/shard_map/while/body/eval_jaxpr/dot_general | solution.py:35
  158.2 0.1 constant_dynamic-slice_fusion.4
  158.3 0.1 constant_dynamic-slice_fusion.5
  158.4 30.9 %select_reduce_fusion.3 = f32[3072,512]{1,0:T(8,128)} fusion(f32[32,512]{1,0:T(8,128)S(1)} %bitcast.50, s32[32,512]{1,0:T(8,128)S(1)} %bitcast.51), kind=kLoop, calls=%fused_computation.clone.1 | loop fusion | flops 149422080 | bytes 6422528 | tf_op jit(solution)/shard_map/while/body/eval_jaxpr/reduce_sum | solution.py:32
  189.3 5.4 %fusion.11 = f32[512]{0:T(512)S(1)} fusion(f32[3072,512]{1,0:T(8,128)} %select_reduce_fusion.3, f32[16,3072]{1,0:T(8,128)S(1)} %get-tuple-element.129, bf16[4,16,512]{2,1,0:T(8,128)(2,1)S(1)} %get-tuple-element.126, s32[]{:T(128)} %get-tuple-element.116), kind=kOutput, calls=%fused_computation.4.clone.1 | convolution fusion | flops 302013952 | bytes 6506500 | tf_op jit(solution)/shard_map/while/body/eval_jaxpr/dot_general | solution.py:35
  194.8 5.9 %all-reduce = f32[2048]{0:T(1024)S(1)} all-reduce(f32[2048]{0:T(1024)S(1)} %bitcast.61), channel_id=2, replica_groups=mesh['col'=8,'lev'=4] {'lev'}, use_global_device_ids=true, to_apply=%region_4.5.clone | all-reduce | flops 2048 | bytes 16384
  200.7 0.1 fusion.3
  200.8 0.1 select_reduce_fusion.1
  200.9 40.3 %psum.7 = f32[32]{0:T(128)} all-reduce(f32[32]{0:T(128)S(1)} %select_reduce_fusion.1), channel_id=1, replica_groups=mesh['col'=8,'lev'=4] {'col','lev'}, use_global_device_ids=true, to_apply=%region_6.7 | all-reduce | flops 32 | bytes 256 | tf_op jit(solution)/shard_map/psum | solution.py:69
  (38 shorter events, 0.4 us)
Async XLA Ops:
  0.6 8.1 %copy-start.2 = (f32[12,1024]{1,0:T(8,128)S(1)}, f32[12,1024]{1,0:T(8,128)}, u32[]{:S(2)}) copy-start(f32[12,1024]{1,0:T(8,128)} %param.11) | copy-start | bytes 147460
  0.6 42.9 %copy-start = (s32[32,2048]{1,0:T(8,128)S(1)}, s32[32,2048]{1,0:T(8,128)}, u32[]{:S(2)}) copy-start(s32[32,2048]{1,0:T(8,128)} %param.14) | copy-start | bytes 786436
  4.4 39.4 %copy-start.1 = (f32[32,2048]{1,0:T(8,128)S(1)}, f32[32,2048]{1,0:T(8,128)}, u32[]{:S(2)}) copy-start(f32[32,2048]{1,0:T(8,128)} %param.13) | copy-start | bytes 786436
  4.4 39.6 %copy-start.3 = (bf16[16,2048]{1,0:T(8,128)(2,1)S(1)}, bf16[16,2048]{1,0:T(8,128)(2,1)}, u32[]{:S(2)}) copy-start(bf16[16,2048]{1,0:T(8,128)(2,1)} %param.12) | copy-start | bytes 196612
  4.4 39.7 %copy-start.8 = (u32[32]{0:T(128)S(1)}, u32[32]{0:T(128)}, u32[]{:S(2)}) copy-start(u32[32]{0:T(128)} %constant.27) | copy-start | bytes 388
  4.4 32.3 %all-to-all-start = ((bf16[12,64,1024]{2,0,1:T(8,128)(2,1)}), bf16[12,64,1024]{2,0,1:T(8,128)(2,1)S(1)}, u32[]{:S(2)}, u32[]{:S(2)}) async-start(bf16[12,64,1024]{2,0,1:T(8,128)(2,1)} %copy.23), calls=%async_computation | async-start | bytes 4194304 | tf_op jit(solution)/shard_map/all_to_all | solution.py:43
  38.0 7.3 %collective-permute-start = (f32[16,1024]{1,0:T(8,128)S(1)}, f32[16,1024]{1,0:T(8,128)S(1)}, u32[]{:S(2)}, u32[]{:S(2)}) collective-permute-start(f32[16,1024]{1,0:T(8,128)S(1)} %bitcast.55), channel_id=1, source_target_pairs={{0,4},{4,8},{8,12},{12,16},{16,20},{20,24},{24,28},{1,5},{5,9},{9,... | collective-permute-start | bytes 196616 | tf_op jit(solution)/shard_map/ppermute | solution.py:20
  42.3 6.2 %collective-permute-start.1 = (f32[16,1024]{1,0:T(8,128)S(1)}, f32[16,1024]{1,0:T(8,128)S(1)}, u32[]{:S(2)}, u32[]{:S(2)}) collective-permute-start(f32[16,1024]{1,0:T(8,128)S(1)} %bitcast.56), channel_id=1, source_target_pairs={{4,0},{8,4},{12,8},{16,12},{20,16},{24,20},{28,24},{5,1},{9,5},{13... | collective-permute-start | bytes 196616 | tf_op jit(solution)/shard_map/ppermute | solution.py:22
  48.4 152.2 %copy-start.5 = (f32[512]{0:T(512)S(1)}, f32[512]{0:T(512)}, u32[]{:S(2)}) copy-start(f32[512]{0:T(512)} %param.15) | copy-start | bytes 6148
  48.4 152.2 %copy-start.6 = (s32[512]{0:T(512)S(1)}, s32[512]{0:T(512)}, u32[]{:S(2)}) copy-start(s32[512]{0:T(512)} %param.17) | copy-start | bytes 6148
  48.5 152.3 %copy-start.7 = (s32[512]{0:T(512)S(1)}, s32[512]{0:T(512)}, u32[]{:S(2)}) copy-start(s32[512]{0:T(512)} %param.16) | copy-start | bytes 6148
  200.7 40.4 %copy-start.4 = (f32[512]{0:T(512)}, f32[512]{0:T(512)S(1)}, u32[]{:S(2)}) copy-start(f32[512]{0:T(512)S(1)} %fusion.3) | copy-start | bytes 6148
where the time goes:
time: 242 us; the launch traced here: 241 us
  other arithmetic  124 us (51%)
  blocking collectives  74.1 us (31%)
  matrix products  21.7 us (9%)
  starting transfers between devices  9.9 us (4%)
  local copies, waits for them, and re-layouts  6.36 us (3%)
  waiting for transfers between devices  3.13 us (1%)
    reduce_sum x4, other arithmetic, block_pairs(): jnp.sum(jnp.where(index[:, None, :] == column_ids[None, :, :], weight[:,...  124 us
    psum x1, blocking collectives, shards(): type_impact = lax.psum(type_part, ('col', 'lev'))  40.3 us
    all_gather x1, blocking collectives, shards(): all_error = lax.all_gather(error_sum, 'lev', axis=0, tiled=True)  27.9 us
    dot_general x4, matrix products, block_pairs(): jnp.dot(extended, table, precision=lax.Precision.HIGHEST, preferred_eleme...  21.7 us
    unnamed x1, blocking collectives  5.87 us
    unnamed x23, local copies, waits for them, and re-layouts  5.23 us
  transfers between devices with their start and end apart: 3, of which 1 were waited for; matrix products, arithmetic and copies ran while one was open for 0% of the time, Pallas kernels for 0%

commit v1 on v0

v1 whole, which is shorter than its diff:
```python
import functools

import jax
import jax.numpy as jnp
from jax import lax
from jax.experimental import pallas as pl
from jax.experimental.pallas import tpu as pltpu
from jax.sharding import PartitionSpec as P

MEMBERS = 64
NTYPE = 32
LANES = 128
MESH = pl.DeviceIdType.MESH


def remote(src, dst, send, recv, target):
    return pltpu.make_async_remote_copy(
        src_ref=src, dst_ref=dst, send_sem=send, recv_sem=recv, device_id=target, device_id_type=MESH
    )


def kernel(
    dims,
    state_hbm, error_hbm, anom_hbm, weight_hbm, index_hbm, innov_hbm, type_hbm, live_hbm,
    impact_ref, total_ref,
    state, error, part, landed, sens, anom, anom_t, weight, index, index_t, innov, kind, live,
    split, table, picked, pair_out, pair_in, type_out, type_in,
    load_sem, quarter_sem, list_sem, anom_sem, own_sem,
    rs_send, rs_recv, an_send, an_recv, me_send, me_recv, ga_send, ga_recv,
    ha_send, ha_recv, fw_send, fw_recv, pa_send, pa_recv, ty_send, ty_recv,
):
    ncol, nlev, nlo, nhi, groups = dims
    quarter = impact_ref.shape[0] * impact_ref.shape[1]
    rows_q = impact_ref.shape[0]
    mq = anom_hbm.shape[0]
    neigh = index_hbm.shape[0]
    go = quarter // rows_q
    columns = state.shape[2]
    levels = state.shape[0]
    hpt = columns // LANES
    total = ncol * nlev

    col = lax.axis_index("col")
    lev = lax.axis_index("lev")
    hi = lev // nlo
    lo = lev % nlo
    me = col * nlev + lev

    copy_err = pltpu.make_async_copy(error_hbm, error, load_sem.at[0])
    copy_err.start()
    state_loads = []
    for d in range(1, nlev + 1):
        q = lax.rem(lev + d, nlev)
        rows = pl.ds(pl.multiple_of(q * mq, mq), mq)
        c = pltpu.make_async_copy(state_hbm.at[:, rows, :], state.at[:, rows, :], quarter_sem.at[d - 1])
        c.start()
        state_loads.append(c)
    list_loads = []
    for g in range(groups):
        h = (g * go) // quarter
        start = (h * nlo + lo) * quarter + (g * go) % quarter
        cols = pl.ds(pl.multiple_of(start, go), go)
        for i, (src, dst) in enumerate(((index_hbm, index), (weight_hbm, weight))):
            c = pltpu.make_async_copy(src.at[:, cols], dst.at[pl.ds(g * neigh, neigh), :], list_sem.at[i, g])
            c.start()
            list_loads.append(c)
    own_loads = []
    for h in range(nhi):
        cols = pl.ds(pl.multiple_of((h * nlo + lo) * quarter, quarter), quarter)
        c = pltpu.make_async_copy(
            anom_hbm.at[:, cols], anom.at[lo, :, pl.ds(h * quarter, quarter)], anom_sem.at[h]
        )
        c.start()
        own_loads.append(c)
    for i, (src, dst) in enumerate(((innov_hbm, innov), (type_hbm, kind), (live_hbm, live))):
        c = pltpu.make_async_copy(src, dst.at[hi], own_sem.at[i])
        c.start()
        own_loads.append(c)

    barrier = pltpu.get_barrier_semaphore()

    def greet(d, carry):
        p = lax.rem(me + d, total)
        pl.semaphore_signal(
            barrier, inc=1, device_id={"col": p // nlev, "lev": lax.rem(p, nlev)}, device_id_type=MESH
        )
        return carry

    lax.fori_loop(1, total, greet, 0)

    copy_err.wait()
    for d in range(1, nlev + 1):
        q = lax.rem(lev + d, nlev)
        rows = pl.ds(pl.multiple_of(q * mq, mq), mq)
        state_loads[d - 1].wait()
        acc = state[0, rows, :].astype(jnp.float32) * error[pl.ds(0, 1), :]
        for l in range(1, levels):
            acc = acc + state[l, rows, :].astype(jnp.float32) * error[pl.ds(l, 1), :]
        part[d - 1] = acc

    pl.semaphore_wait(barrier, total - 1)

    scatter = []
    for d in range(1, nlev):
        q = lax.rem(lev + d, nlev)
        c = remote(part.at[d - 1], landed.at[d - 1], rs_send.at[d - 1], rs_recv.at[d - 1], {"lev": q})
        c.start()
        scatter.append(c)
    anom_sends = []
    for d in range(1, nlo):
        other = lax.rem(lo + d, nlo)
        for h in range(nhi):
            cols = pl.ds(pl.multiple_of((h * nlo + other) * quarter, quarter), quarter)
            c = remote(
                anom_hbm.at[:, cols], anom.at[lo, :, pl.ds(h * quarter, quarter)],
                an_send.at[d - 1, h], an_recv.at[d - 1, h], {"lev": hi * nlo + other},
            )
            c.start()
            anom_sends.append(c)
    meta_sends = []
    for d in range(1, nhi):
        other = lax.rem(hi + d, nhi)
        for i, (src, dst) in enumerate(((innov_hbm, innov), (type_hbm, kind), (live_hbm, live))):
            c = remote(src, dst.at[hi], me_send.at[d - 1, i], me_recv.at[d - 1, i], {"lev": other * nlo + lo})
            c.start()
            meta_sends.append(c)

    for c in list_loads:
        c.wait()
    index_t[...] = index[...].T
    picked[...] = jnp.zeros_like(picked)

    for c in scatter:
        c.wait_recv()
    summed = part[nlev - 1]
    for d in range(1, nlev):
        summed = summed + landed[d - 1]
    sens[1, lo] = summed

    left = {"col": jnp.maximum(col - 1, 0)}
    right = {"col": jnp.minimum(col + 1, ncol - 1)}
    to_left = remote(sens.at[1, lo], sens.at[2, lo], ha_send.at[0], ha_recv.at[1], left)
    to_right = remote(sens.at[1, lo], sens.at[0, lo], ha_send.at[1], ha_recv.at[0], right)
    has_left = col > 0
    has_right = col < ncol - 1
    pl.when(has_left)(to_left.start)
    pl.when(has_right)(to_right.start)
    gather = []
    for d in range(1, nlo):
        other = lax.rem(lo + d, nlo)
        c = remote(sens.at[1, lo], sens.at[1, lo], ga_send.at[d - 1], ga_recv.at[d - 1], {"lev": hi * nlo + other})
        c.start()
        gather.append(c)

    for c in own_loads:
        c.wait()
    for c in anom_sends:
        c.wait_recv()
    members = nlo * mq
    parts = 3
    depth = anom_t.shape[1]
    flat = anom[...].reshape(members, anom.shape[2]).astype(jnp.float32)
    pieces = [flat] * parts
    if depth > parts * members:
        pieces.append(jnp.zeros((depth - parts * members, anom.shape[2]), jnp.float32))
        split[pl.ds(parts * members, depth - parts * members), :] = jnp.zeros(
            (depth - parts * members, columns), jnp.bfloat16
        )
    anom_t[...] = jnp.concatenate(pieces, axis=0).T.astype(jnp.bfloat16)

    lane_group = lax.broadcasted_iota(jnp.int32, (8, LANES), 1) // neigh

    def tile(j):
        rest = sens[j].reshape(members, columns)
        for i in range(parts):
            piece = rest.astype(jnp.bfloat16)
            split[pl.ds(i * members, members), :] = piece
            rest = rest - piece.astype(jnp.float32)
        for g in range(groups):
            table[g % 2] = jnp.dot(
                anom_t[pl.ds(g * go, go), :], split[...], preferred_element_type=jnp.float32
            )

            def pick(r, carry):
                for u in range(4):
                    rows = pl.ds(pl.multiple_of(r * 32 + u * 8, 8), 8)
                    where = index_t[rows, :]
                    lane = where & (LANES - 1)
                    block = jnp.where(lane_group == g, where >> 7, -1)
                    acc = picked[rows, :]
                    for h in range(hpt):
                        got = jnp.take_along_axis(
                            table[g % 2, rows, pl.ds(h * LANES, LANES)], lane, axis=1, mode="promise_in_bounds"
                        )
                        acc = jnp.where(block == j * hpt + h, got, acc)
                    picked[rows, :] = acc
                return carry

            lax.fori_loop(0, go // 32, pick, 0)

    for c in gather:
        c.wait_recv()
    tile(1)

    forwards = []
    for side, here in ((0, has_left), (2, has_right)):
        copies = []
        for d in range(1, nlo):
            other = lax.rem(lo + d, nlo)
            copies.append(
                remote(
                    sens.at[side, lo], sens.at[side, lo], fw_send.at[d - 1, side // 2],
                    fw_recv.at[d - 1, side // 2], {"lev": hi * nlo + other},
                )
            )
        forwards.append((side, here, copies))
    for side, here, copies in forwards:
        @pl.when(here)
        def _():
            (to_right if side == 0 else to_left).wait_recv()
            for c in copies:
                c.start()
    for side, here, copies in forwards:
        @pl.when(here)
        def _():
            for c in copies:
                c.wait_recv()
            tile(side)

    pair = (picked[...].T * weight[...]).reshape(groups, neigh, go).sum(axis=1)
    pair_out[...] = pair.reshape(nhi, rows_q, go)
    pair_sends = []
    for d in range(1, nhi):
        other = lax.rem(hi + d, nhi)
        c = remote(
            pair_out.at[other], pair_in.at[d - 1], pa_send.at[d - 1], pa_recv.at[d - 1], {"lev": other * nlo + lo}
        )
        c.start()
        pair_sends.append(c)

    for c in meta_sends:
        c.wait_recv()
    ids = lax.broadcasted_iota(jnp.int32, (NTYPE, go), 0)
    binned = jnp.zeros((NTYPE, go), jnp.float32)
    for h in range(nhi):
        share = pair_out[h] * innov[h] * live[h].astype(jnp.float32) / (MEMBERS - 1.0)
        kinds = kind[h]
        for r in range(rows_q):
            binned = binned + jnp.where(ids == kinds[r:r + 1, :], share[r:r + 1, :], 0.0)
    folded = binned[:, :LANES]
    for b in range(1, go // LANES):
        folded = folded + binned[:, b * LANES:(b + 1) * LANES]
    square = jnp.concatenate([folded, jnp.zeros((LANES - NTYPE, LANES), jnp.float32)], axis=0)
    type_row = jnp.sum(square.T, axis=0, keepdims=True)
    type_out[...] = type_row
    type_in[me] = type_row

    def spread(d, carry):
        p = lax.rem(me + d, total)
        remote(
            type_out, type_in.at[me], ty_send.at[0], ty_recv.at[0], {"col": p // nlev, "lev": lax.rem(p, nlev)}
        ).start()
        return carry

    lax.fori_loop(1, total, spread, 0)

    for c in pair_sends:
        c.wait_recv()
    whole = pair_out[hi]
    for d in range(1, nhi):
        whole = whole + pair_in[d - 1]
    impact_ref[...] = whole * innov[hi] * live[hi].astype(jnp.float32) / (MEMBERS - 1.0)

    everyone = remote(
        type_in.at[pl.ds(0, total - 1)], type_in.at[pl.ds(0, total - 1)], ty_send.at[0], ty_recv.at[0], {"lev": lev}
    )
    everyone.wait_recv()
    total_ref[...] = jnp.sum(type_in[...], axis=0)

    for c in scatter + anom_sends + meta_sends + gather + pair_sends:
        c.wait_send()
    pl.when(has_left)(to_left.wait_send)
    pl.when(has_right)(to_right.wait_send)
    for side, here, copies in forwards:
        @pl.when(here)
        def _():
            for c in copies:
                c.wait_send()
    everyone.wait_send()


def shards(state_anom, error_sum, obs_anom, local_weight, neighbours, innovation, obs_type, live):
    ncol, nlev = lax.axis_size("col"), lax.axis_size("lev")
    nlo = 2 if nlev % 2 == 0 else 1
    nhi = nlev // nlo
    levels, members, columns = state_anom.shape
    mq, obs_slots = obs_anom.shape
    neigh = local_weight.shape[0]
    quarter = innovation.shape[0]
    handled = quarter * nhi
    groups = LANES // neigh
    go = handled // groups
    rows_q = quarter // go
    half = nlo * mq
    depth = -(-3 * half // LANES) * LANES
    total = ncol * nlev
    dma = pltpu.SemaphoreType.DMA
    f32, bf16, i32 = jnp.float32, jnp.bfloat16, jnp.int32
    vm = pltpu.VMEM
    scratch = [
        vm((levels, members, columns), bf16), vm((levels, columns), f32), vm((nlev, mq, columns), f32),
        vm((max(nlev - 1, 1), mq, columns), f32), vm((3, nlo, mq, columns), f32), vm((nlo, mq, handled), bf16),
        vm((handled, depth), bf16), vm((LANES, go), f32), vm((LANES, go), i32), vm((go, LANES), i32),
        vm((nhi, rows_q, go), f32), vm((nhi, rows_q, go), i32), vm((nhi, rows_q, go), i32),
        vm((depth, columns), bf16), vm((2, go, columns), f32), vm((go, LANES), f32),
        vm((nhi, rows_q, go), f32), vm((max(nhi - 1, 1), rows_q, go), f32),
        vm((1, LANES), f32), vm((total, 1, LANES), f32),
        dma((1,)), dma((nlev,)), dma((2, groups)), dma((nhi,)), dma((3,)),
        dma((nlev,)), dma((nlev,)), dma((nlo, nhi)), dma((nlo, nhi)), dma((nhi, 3)), dma((nhi, 3)),
        dma((nlo,)), dma((nlo,)), dma((2,)), dma((2,)), dma((nlo, 2)), dma((nlo, 2)),
        dma((nhi,)), dma((nhi,)), dma((1,)), dma((1,)),
    ]
    anywhere = pl.BlockSpec(memory_space=pl.ANY)
    impact, totals = pl.pallas_call(
        functools.partial(kernel, (ncol, nlev, nlo, nhi, groups)),
        out_shape=(jax.ShapeDtypeStruct((rows_q, go), f32), jax.ShapeDtypeStruct((1, LANES), f32)),
        in_specs=[anywhere] * 8,
        out_specs=(pl.BlockSpec(memory_space=pltpu.VMEM), pl.BlockSpec(memory_space=pltpu.VMEM)),
        scratch_shapes=scratch,
        compiler_params=pltpu.CompilerParams(collective_id=0, has_side_effects=True),
    )(
        state_anom, error_sum, obs_anom, local_weight, neighbours,
        innovation.reshape(rows_q, go), obs_type.reshape(rows_q, go), live.reshape(rows_q, go),
    )
    return impact.reshape(quarter), totals[0, :NTYPE]


def solution(mesh):
    in_specs = (
        P("lev", None, "col"),
        P("lev", "col"),
        P("lev", "col"),
        P(None, "col"),
        P(None, "col"),
        P(("col", "lev")),
        P(("col", "lev")),
        P(("col", "lev")),
    )
    out_specs = (P(("col", "lev")), P())
    return jax.shard_map(shards, mesh=mesh, in_specs=in_specs, out_specs=out_specs, check_vma=False)
```

time: 242 us -> 40.6 us (0.17)
  other arithmetic: 124 us -> 0 us
  blocking collectives: 74.1 us -> 0 us
  Pallas kernels: 0 us -> 33.5 us
  matrix products: 21.7 us -> 0 us
  starting transfers between devices: 9.9 us -> 0 us
  waiting for transfers between devices: 3.13 us -> 0 us
    reduce_sum x5 -> x0, other arithmetic: 124 us -> none  [the longest x4 124 us: block_pairs(): jnp.sum(jnp.where(index[:, None, :] == column_ids[None, :, :], weight[:,...]
    psum x1 -> x0, blocking collectives: 40.3 us -> none  [shards(): type_impact = lax.psum(type_part, ('col', 'lev'))]
    pallas_call x0 -> x1, Pallas kernels: none -> 33.5 us  [shards(): pl.pallas_call(functools.partial(kernel, (ncol, nlev, nlo, nhi, groups)),...]
    all_gather x1 -> x0, blocking collectives: 27.9 us -> none  [shards(): all_error = lax.all_gather(error_sum, 'lev', axis=0, tiled=True)]
    dot_general x4 -> x0, matrix products: 21.7 us -> none  [block_pairs(): jnp.dot(extended, table, precision=lax.Precision.HIGHEST, preferred_eleme...]
    unnamed x1 -> x0, blocking collectives: 5.87 us -> none
    ppermute x2 -> x0, starting transfers between devices: 5.53 us -> none  [the longest x1 4.24 us: with_halo(): lax.ppermute(tail, axis, [(i, (i + 1) % count) for i in range(ends)])]
    all_to_all x1 -> x0, starting transfers between devices: 4.37 us -> none  [shards(): lax.all_to_all(state_anom, 'lev', split_axis=1, concat_axis=0, tiled=True)]
  transfers between devices with their start and end apart: 3 -> 0, of which waited for: 1 -> 0; matrix products, arithmetic and copies ran while one was open for 0% -> 0% of each run, Pallas kernels for 0% -> 0%
where the time goes in v1:
time: 40.6 us; the launch traced here: 40.4 us
  Pallas kernels  33.5 us (83%)
  local copies, waits for them, and re-layouts  6.2 us (15%)
  between operations  0.64 us (2%)
    pallas_call x1, Pallas kernels, shards(): pl.pallas_call(functools.partial(kernel, (ncol, nlev, nlo, nhi, groups)),...  33.5 us
    reshape x1, local copies, waits for them, and re-layouts, shards(): obs_type.reshape(rows_q, go)  1.28 us
    reshape x1, local copies, waits for them, and re-layouts, shards(): innovation.reshape(rows_q, go)  1.27 us
    reshape x1, local copies, waits for them, and re-layouts, shards(): live.reshape(rows_q, go)  1.25 us
    unnamed x1, local copies, waits for them, and re-layouts  1.25 us
    squeeze x1, local copies, waits for them, and re-layouts, shards(): return (impact.reshape(quarter), totals[0, :NTYPE])  1.14 us

profile of v1, /device:TPU:0, one launch (start us, length us, event | category | flops | bytes accessed | tf_op | source)
XLA Modules:
  0.0 40.4 jit_solution(5198806342616137295)
XLA Ops:
  0.6 1.3 %reshape.16.innov_hbm = f32[2,256]{1,0:T(2,128)} reshape(f32[512]{0:T(512)} %param.13) | data formatting | bytes 4096 | tf_op jit(solution)/shard_map/reshape | solution.py:333
  1.9 1.3 %reshape.17.type_hbm = s32[2,256]{1,0:T(2,128)} reshape(s32[512]{0:T(512)} %param.14) | data formatting | bytes 4096 | tf_op jit(solution)/shard_map/reshape | solution.py:333
  3.2 1.3 %reshape.18.live_hbm = s32[2,256]{1,0:T(2,128)} reshape(s32[512]{0:T(512)} %param.15) | data formatting | bytes 4096 | tf_op jit(solution)/shard_map/reshape | solution.py:333
  4.4 33.5 %shard_map.95 = (f32[2,256]{1,0:T(2,128)}, f32[1,128]{1,0:T(1,128)}) custom-call(bf16[12,64,1024]{2,1,0:T(8,128)(2,1)} %state_hbm.1, f32[12,1024]{1,0:T(8,128)} %error_hbm.1, bf16[16,2048]{1,0:T(8,128)(2,1)} %anom_hbm.1, f32[32,2048]{1,0:T(8,128)} %weight_hbm.1, s32[32,2048]{1,0:T(8,128)} %index_hbm.1, f32[2,256]{1,0:T(2,128)} %reshape.16.innov_hbm, ...), custom_call_target="tpu_custom_call" | custom-call | tf_op jit(solution)/shard_map/pallas_call | solution.py:324
  38.0 1.2 %copy.10 = f32[1,2,2,128]{3,1,2,0:T(2,128)} copy(f32[1,2,2,128]{3,2,1,0:T(2,128)} %bitcast.5) | data formatting | bytes 4096
  39.2 1.1 %slice_bitcast_fusion = f32[32]{0:T(128)} fusion(f32[1,128]{1,0:T(1,128)} %get-tuple-element.5), kind=kLoop, calls=%fused_computation | loop fusion | bytes 256 | tf_op jit(solution)/shard_map/squeeze | solution.py:335

commit v2 on v1

--- a/solution.py
+++ b/solution.py
@@ -30,11 +30,11 @@
     ha_send, ha_recv, fw_send, fw_recv, pa_send, pa_recv, ty_send, ty_recv,
 ):
     ncol, nlev, nlo, nhi, groups = dims
-    quarter = impact_ref.shape[0] * impact_ref.shape[1]
-    rows_q = impact_ref.shape[0]
+    quarter = impact_ref.shape[1]
     mq = anom_hbm.shape[0]
     neigh = index_hbm.shape[0]
-    go = quarter // rows_q
+    go = index.shape[1]
+    rows_q = quarter // go
     columns = state.shape[2]
     levels = state.shape[0]
     hpt = columns // LANES
@@ -177,26 +177,26 @@
             split[pl.ds(i * members, members), :] = piece
             rest = rest - piece.astype(jnp.float32)
         for g in range(groups):
-            table[g % 2] = jnp.dot(
-                anom_t[pl.ds(g * go, go), :], split[...], preferred_element_type=jnp.float32
-            )
-
-            def pick(r, carry):
-                for u in range(4):
-                    rows = pl.ds(pl.multiple_of(r * 32 + u * 8, 8), 8)
-                    where = index_t[rows, :]
-                    lane = where & (LANES - 1)
-                    block = jnp.where(lane_group == g, where >> 7, -1)
-                    acc = picked[rows, :]
+            table[g] = jnp.dot(anom_t[pl.ds(g * go, go), :], split[...], preferred_element_type=jnp.float32)
+
+        def pick(r, carry):
+            for u in range(2):
+                rows = pl.ds(pl.multiple_of(r * 16 + u * 8, 8), 8)
+                where = index_t[rows, :]
+                lane = where & (LANES - 1)
+                block = where >> 7
+                acc = picked[rows, :]
+                for g in range(groups):
+                    mine = jnp.where(lane_group == g, block, -1)
                     for h in range(hpt):
                         got = jnp.take_along_axis(
-                            table[g % 2, rows, pl.ds(h * LANES, LANES)], lane, axis=1, mode="promise_in_bounds"
+                            table[g, rows, pl.ds(h * LANES, LANES)], lane, axis=1, mode="promise_in_bounds"
                         )
-                        acc = jnp.where(block == j * hpt + h, got, acc)
-                    picked[rows, :] = acc
-                return carry
-
-            lax.fori_loop(0, go // 32, pick, 0)
+                        acc = jnp.where(mine == j * hpt + h, got, acc)
+                picked[rows, :] = acc
+            return carry
+
+        lax.fori_loop(0, go // 16, pick, 0)
 
     for c in gather:
         c.wait_recv()
@@ -228,7 +228,8 @@
             tile(side)
 
     pair = (picked[...].T * weight[...]).reshape(groups, neigh, go).sum(axis=1)
-    pair_out[...] = pair.reshape(nhi, rows_q, go)
+    for h in range(nhi):
+        pair_out[h] = jnp.concatenate([pair[h * rows_q + r:h * rows_q + r + 1] for r in range(rows_q)], axis=1)
     pair_sends = []
     for d in range(1, nhi):
         other = lax.rem(hi + d, nhi)
@@ -240,15 +241,13 @@
 
     for c in meta_sends:
         c.wait_recv()
-    ids = lax.broadcasted_iota(jnp.int32, (NTYPE, go), 0)
-    binned = jnp.zeros((NTYPE, go), jnp.float32)
+    ids = lax.broadcasted_iota(jnp.int32, (NTYPE, quarter), 0)
+    binned = jnp.zeros((NTYPE, quarter), jnp.float32)
     for h in range(nhi):
         share = pair_out[h] * innov[h] * live[h].astype(jnp.float32) / (MEMBERS - 1.0)
-        kinds = kind[h]
-        for r in range(rows_q):
-            binned = binned + jnp.where(ids == kinds[r:r + 1, :], share[r:r + 1, :], 0.0)
+        binned = binned + jnp.where(ids == kind[h], share, 0.0)
     folded = binned[:, :LANES]
-    for b in range(1, go // LANES):
+    for b in range(1, quarter // LANES):
         folded = folded + binned[:, b * LANES:(b + 1) * LANES]
     square = jnp.concatenate([folded, jnp.zeros((LANES - NTYPE, LANES), jnp.float32)], axis=0)
     type_row = jnp.sum(square.T, axis=0, keepdims=True)
@@ -300,7 +299,6 @@
     handled = quarter * nhi
     groups = LANES // neigh
     go = handled // groups
-    rows_q = quarter // go
     half = nlo * mq
     depth = -(-3 * half // LANES) * LANES
     total = ncol * nlev
@@ -311,9 +309,9 @@
         vm((levels, members, columns), bf16), vm((levels, columns), f32), vm((nlev, mq, columns), f32),
         vm((max(nlev - 1, 1), mq, columns), f32), vm((3, nlo, mq, columns), f32), vm((nlo, mq, handled), bf16),
         vm((handled, depth), bf16), vm((LANES, go), f32), vm((LANES, go), i32), vm((go, LANES), i32),
-        vm((nhi, rows_q, go), f32), vm((nhi, rows_q, go), i32), vm((nhi, rows_q, go), i32),
-        vm((depth, columns), bf16), vm((2, go, columns), f32), vm((go, LANES), f32),
-        vm((nhi, rows_q, go), f32), vm((max(nhi - 1, 1), rows_q, go), f32),
+        vm((nhi, 1, quarter), f32), vm((nhi, 1, quarter), i32), vm((nhi, 1, quarter), i32),
+        vm((depth, columns), bf16), vm((groups, go, columns), f32), vm((go, LANES), f32),
+        vm((nhi, 1, quarter), f32), vm((max(nhi - 1, 1), 1, quarter), f32),
         vm((1, LANES), f32), vm((total, 1, LANES), f32),
         dma((1,)), dma((nlev,)), dma((2, groups)), dma((nhi,)), dma((3,)),
         dma((nlev,)), dma((nlev,)), dma((nlo, nhi)), dma((nlo, nhi)), dma((nhi, 3)), dma((nhi, 3)),
@@ -323,14 +321,14 @@
     anywhere = pl.BlockSpec(memory_space=pl.ANY)
     impact, totals = pl.pallas_call(
         functools.partial(kernel, (ncol, nlev, nlo, nhi, groups)),
-        out_shape=(jax.ShapeDtypeStruct((rows_q, go), f32), jax.ShapeDtypeStruct((1, LANES), f32)),
+        out_shape=(jax.ShapeDtypeStruct((1, quarter), f32), jax.ShapeDtypeStruct((1, LANES), f32)),
         in_specs=[anywhere] * 8,
         out_specs=(pl.BlockSpec(memory_space=pltpu.VMEM), pl.BlockSpec(memory_space=pltpu.VMEM)),
         scratch_shapes=scratch,
         compiler_params=pltpu.CompilerParams(collective_id=0, has_side_effects=True),
     )(
         state_anom, error_sum, obs_anom, local_weight, neighbours,
-        innovation.reshape(rows_q, go), obs_type.reshape(rows_q, go), live.reshape(rows_q, go),
+        innovation.reshape(1, quarter), obs_type.reshape(1, quarter), live.reshape(1, quarter),
     )
     return impact.reshape(quarter), totals[0, :NTYPE]
 

time: 40.6 us -> 31.3 us (0.77)
  Pallas kernels: 33.5 us -> 28.1 us
  local copies, waits for them, and re-layouts: 6.2 us -> 2.39 us
    pallas_call x1, Pallas kernels: 33.5 us -> 28.1 us  [shards(): pl.pallas_call(functools.partial(kernel, (ncol, nlev, nlo, nhi, groups)),...]
    reshape x3 -> x0, local copies, waits for them, and re-layouts: 3.8 us -> none  [the longest x1 1.28 us: shards(): obs_type.reshape(rows_q, go)]
where the time goes in v2:
time: 31.3 us; the launch traced here: 31.2 us
  Pallas kernels  28.1 us (90%)
  local copies, waits for them, and re-layouts  2.39 us (8%)
  between operations  0.64 us (2%)
    pallas_call x1, Pallas kernels, shards(): pl.pallas_call(functools.partial(kernel, (ncol, nlev, nlo, nhi, groups)),...  28.1 us
    unnamed x1, local copies, waits for them, and re-layouts  1.25 us
    squeeze x1, local copies, waits for them, and re-layouts, shards(): return (impact.reshape(quarter), totals[0, :NTYPE])  1.14 us

profile of v2, /device:TPU:0, one launch (start us, length us, event | category | flops | bytes accessed | tf_op | source)
XLA Modules:
  0.0 31.2 jit_solution(12791159528302584579)
XLA Ops:
  0.6 28.1 %shard_map.95 = (f32[1,512]{1,0:T(1,128)}, f32[1,128]{1,0:T(1,128)}) custom-call(bf16[12,64,1024]{2,1,0:T(8,128)(2,1)} %state_hbm.1, f32[12,1024]{1,0:T(8,128)} %error_hbm.1, bf16[16,2048]{1,0:T(8,128)(2,1)} %anom_hbm.1, f32[32,2048]{1,0:T(8,128)} %weight_hbm.1, s32[32,2048]{1,0:T(8,128)} %index_hbm.1, f32[1,512]{1,0:T(1,128)} %bitcast.6, s32[1,512]{1,0:T(1,128)} %bitcast.7, ...), custom_call_target="tpu_custom_call" | custom-call | tf_op jit(solution)/shard_map/pallas_call | solution.py:322
  28.8 1.1 %slice_bitcast_fusion = f32[32]{0:T(128)} fusion(f32[1,128]{1,0:T(1,128)} %get-tuple-element.5), kind=kLoop, calls=%fused_computation | loop fusion | bytes 256 | tf_op jit(solution)/shard_map/squeeze | solution.py:333
  29.9 1.2 %copy.11 = f32[512]{0:T(512)} copy(f32[512]{0:T(512)} %bitcast.9) | data formatting | bytes 4096

commit v3 on v2

--- a/solution.py
+++ b/solution.py
@@ -25,11 +25,11 @@
     impact_ref, total_ref,
     state, error, part, landed, sens, anom, anom_t, weight, index, index_t, innov, kind, live,
     split, table, picked, pair_out, pair_in, type_out, type_in,
-    load_sem, quarter_sem, list_sem, anom_sem, own_sem,
+    word, load_sem, quarter_sem, list_sem, anom_sem, own_sem,
     rs_send, rs_recv, an_send, an_recv, me_send, me_recv, ga_send, ga_recv,
     ha_send, ha_recv, fw_send, fw_recv, pa_send, pa_recv, ty_send, ty_recv,
 ):
-    ncol, nlev, nlo, nhi, groups = dims
+    ncol, nlev, nlo, nhi, groups, chunks = dims
     quarter = impact_ref.shape[1]
     mq = anom_hbm.shape[0]
     neigh = index_hbm.shape[0]
@@ -39,6 +39,8 @@
     levels = state.shape[0]
     hpt = columns // LANES
     total = ncol * nlev
+    width = columns // chunks
+    spans = [pl.ds(c * width, width) for c in range(chunks)]
 
     col = lax.axis_index("col")
     lev = lax.axis_index("lev")
@@ -46,13 +48,44 @@
     lo = lev % nlo
     me = col * nlev + lev
 
+    def visit(act):
+        def one(dc):
+            c = col + dc
+            c = jnp.where(c >= ncol, c - ncol, c)
+            for dl in range(nlev):
+                l = lev + dl
+                act(c, jnp.where(l >= nlev, l - nlev, l))
+
+        if ncol <= 8:
+            for dc in range(ncol - 1, 0, -1):
+                one(dc)
+        else:
+            lax.fori_loop(1, ncol, lambda dc, carry: (one(dc), carry)[1], 0)
+        for dl in range(1, nlev):
+            l = lev + dl
+            act(col, jnp.where(l >= nlev, l - nlev, l))
+
+    barrier = pltpu.get_barrier_semaphore()
+    for d in range(1, nlev):
+        pl.semaphore_signal(barrier, inc=1, device_id={"lev": lax.rem(lev + d, nlev)}, device_id_type=MESH)
+
+    def hail(sem, reach):
+        for here, there in ((col >= reach, col - reach), (col < ncol - reach, col + reach)):
+            @pl.when(here)
+            def _():
+                pl.semaphore_signal(sem, inc=1, device_id={"col": there}, device_id_type=MESH)
+
+    def heard(reach):
+        return jnp.where(col >= reach, 1, 0) + jnp.where(col < ncol - reach, 1, 0)
+
+    hail(barrier, 1)
+    rounds = max(1, (ncol - 1).bit_length())
+
     copy_err = pltpu.make_async_copy(error_hbm, error, load_sem.at[0])
     copy_err.start()
     state_loads = []
-    for d in range(1, nlev + 1):
-        q = lax.rem(lev + d, nlev)
-        rows = pl.ds(pl.multiple_of(q * mq, mq), mq)
-        c = pltpu.make_async_copy(state_hbm.at[:, rows, :], state.at[:, rows, :], quarter_sem.at[d - 1])
+    for k, span in enumerate(spans):
+        c = pltpu.make_async_copy(state_hbm.at[:, :, span], state.at[:, :, span], quarter_sem.at[k])
         c.start()
         state_loads.append(c)
     list_loads = []
@@ -77,35 +110,28 @@
         c.start()
         own_loads.append(c)
 
-    barrier = pltpu.get_barrier_semaphore()
-
-    def greet(d, carry):
-        p = lax.rem(me + d, total)
-        pl.semaphore_signal(
-            barrier, inc=1, device_id={"col": p // nlev, "lev": lax.rem(p, nlev)}, device_id_type=MESH
-        )
-        return carry
-
-    lax.fori_loop(1, total, greet, 0)
-
     copy_err.wait()
-    for d in range(1, nlev + 1):
-        q = lax.rem(lev + d, nlev)
-        rows = pl.ds(pl.multiple_of(q * mq, mq), mq)
-        state_loads[d - 1].wait()
-        acc = state[0, rows, :].astype(jnp.float32) * error[pl.ds(0, 1), :]
-        for l in range(1, levels):
-            acc = acc + state[l, rows, :].astype(jnp.float32) * error[pl.ds(l, 1), :]
-        part[d - 1] = acc
-
-    pl.semaphore_wait(barrier, total - 1)
-
     scatter = []
-    for d in range(1, nlev):
-        q = lax.rem(lev + d, nlev)
-        c = remote(part.at[d - 1], landed.at[d - 1], rs_send.at[d - 1], rs_recv.at[d - 1], {"lev": q})
-        c.start()
-        scatter.append(c)
+    for k, span in enumerate(spans):
+        state_loads[k].wait()
+        for b in range(width // LANES):
+            lanes = pl.ds(k * width + b * LANES, LANES)
+            acc = state[0, :, lanes].astype(jnp.float32) * error[pl.ds(0, 1), lanes]
+            for l in range(1, levels):
+                acc = acc + state[l, :, lanes].astype(jnp.float32) * error[pl.ds(l, 1), lanes]
+            part[:, :, lanes] = acc.reshape(nlev, mq, LANES)
+        if k == 0:
+            pl.semaphore_wait(barrier, nlev - 1 + heard(1))
+            hail(word.at[0], 1)
+        sends = []
+        for d in range(1, nlev):
+            q = lax.rem(lev + d, nlev)
+            c = remote(
+                part.at[q, :, span], landed.at[d - 1, :, span], rs_send.at[d - 1, k], rs_recv.at[d - 1, k], {"lev": q}
+            )
+            c.start()
+            sends.append(c)
+        scatter.append(sends)
     anom_sends = []
     for d in range(1, nlo):
         other = lax.rem(lo + d, nlo)
@@ -130,27 +156,32 @@
     index_t[...] = index[...].T
     picked[...] = jnp.zeros_like(picked)
 
-    for c in scatter:
-        c.wait_recv()
-    summed = part[nlev - 1]
-    for d in range(1, nlev):
-        summed = summed + landed[d - 1]
-    sens[1, lo] = summed
-
     left = {"col": jnp.maximum(col - 1, 0)}
     right = {"col": jnp.minimum(col + 1, ncol - 1)}
-    to_left = remote(sens.at[1, lo], sens.at[2, lo], ha_send.at[0], ha_recv.at[1], left)
-    to_right = remote(sens.at[1, lo], sens.at[0, lo], ha_send.at[1], ha_recv.at[0], right)
     has_left = col > 0
     has_right = col < ncol - 1
-    pl.when(has_left)(to_left.start)
-    pl.when(has_right)(to_right.start)
+    partners = [hi * nlo + lax.rem(lo + d, nlo) for d in range(1, nlo)]
+    halo = []
     gather = []
-    for d in range(1, nlo):
-        other = lax.rem(lo + d, nlo)
-        c = remote(sens.at[1, lo], sens.at[1, lo], ga_send.at[d - 1], ga_recv.at[d - 1], {"lev": hi * nlo + other})
-        c.start()
-        gather.append(c)
+    for k, span in enumerate(spans):
+        for c in scatter[k]:
+            c.wait_recv()
+        summed = part[lev, :, span]
+        for d in range(1, nlev):
+            summed = summed + landed[d - 1, :, span]
+        sens[1, lo, :, span] = summed
+        mine = sens.at[1, lo, :, span]
+        to_left = remote(mine, sens.at[2, lo, :, span], ha_send.at[0, k], ha_recv.at[1, k], left)
+        to_right = remote(mine, sens.at[0, lo, :, span], ha_send.at[1, k], ha_recv.at[0, k], right)
+        pl.when(has_left)(to_left.start)
+        pl.when(has_right)(to_right.start)
+        halo.append((to_left, to_right))
+        copies = []
+        for d, partner in enumerate(partners):
+            c = remote(mine, mine, ga_send.at[d, k], ga_recv.at[d, k], {"lev": partner})
+            c.start()
+            copies.append(c)
+        gather.append(copies)
 
     for c in own_loads:
         c.wait()
@@ -164,68 +195,83 @@
     if depth > parts * members:
         pieces.append(jnp.zeros((depth - parts * members, anom.shape[2]), jnp.float32))
         split[pl.ds(parts * members, depth - parts * members), :] = jnp.zeros(
-            (depth - parts * members, columns), jnp.bfloat16
+            (depth - parts * members, width), jnp.bfloat16
         )
     anom_t[...] = jnp.concatenate(pieces, axis=0).T.astype(jnp.bfloat16)
 
     lane_group = lax.broadcasted_iota(jnp.int32, (8, LANES), 1) // neigh
 
-    def tile(j):
-        rest = sens[j].reshape(members, columns)
+    def tile(j, k):
+        rest = sens[j, :, :, spans[k]].reshape(members, width)
         for i in range(parts):
             piece = rest.astype(jnp.bfloat16)
             split[pl.ds(i * members, members), :] = piece
             rest = rest - piece.astype(jnp.float32)
         for g in range(groups):
             table[g] = jnp.dot(anom_t[pl.ds(g * go, go), :], split[...], preferred_element_type=jnp.float32)
+        first = j * hpt + k * (width // LANES)
 
         def pick(r, carry):
-            for u in range(2):
-                rows = pl.ds(pl.multiple_of(r * 16 + u * 8, 8), 8)
+            for u in range(8):
+                rows = pl.ds(pl.multiple_of(r * 64 + u * 8, 8), 8)
                 where = index_t[rows, :]
                 lane = where & (LANES - 1)
                 block = where >> 7
                 acc = picked[rows, :]
                 for g in range(groups):
                     mine = jnp.where(lane_group == g, block, -1)
-                    for h in range(hpt):
+                    for h in range(width // LANES):
                         got = jnp.take_along_axis(
                             table[g, rows, pl.ds(h * LANES, LANES)], lane, axis=1, mode="promise_in_bounds"
                         )
-                        acc = jnp.where(mine == j * hpt + h, got, acc)
+                        acc = jnp.where(mine == first + h, got, acc)
                 picked[rows, :] = acc
             return carry
 
-        lax.fori_loop(0, go // 16, pick, 0)
-
-    for c in gather:
-        c.wait_recv()
-    tile(1)
+        lax.fori_loop(0, go // 64, pick, 0)
 
     forwards = []
-    for side, here in ((0, has_left), (2, has_right)):
-        copies = []
-        for d in range(1, nlo):
-            other = lax.rem(lo + d, nlo)
-            copies.append(
-                remote(
-                    sens.at[side, lo], sens.at[side, lo], fw_send.at[d - 1, side // 2],
-                    fw_recv.at[d - 1, side // 2], {"lev": hi * nlo + other},
+    for k, span in enumerate(spans):
+        for side, here in ((0, has_left), (2, has_right)):
+            copies = []
+            for d, partner in enumerate(partners):
+                landing = sens.at[side, lo, :, span]
+                copies.append(
+                    remote(landing, landing, fw_send.at[d, side, k], fw_recv.at[d, side, k], {"lev": partner})
                 )
-            )
-        forwards.append((side, here, copies))
-    for side, here, copies in forwards:
-        @pl.when(here)
-        def _():
-            (to_right if side == 0 else to_left).wait_recv()
-            for c in copies:
-                c.start()
-    for side, here, copies in forwards:
+            forwards.append((side, here, copies, k))
+
+    def forward(k):
+        for side, here, copies, at in forwards:
+            if at == k:
+                @pl.when(here)
+                def _():
+                    halo[k][1 if side == 0 else 0].wait_recv()
+                    for c in copies:
+                        c.start()
+
+    def relay(i):
+        if i < rounds:
+            pl.semaphore_wait(word.at[i], heard(1 << i))
+            if i + 1 < rounds:
+                hail(word.at[i + 1], 1 << (i + 1))
+
+    relay(0)
+    for k in range(chunks):
+        for c in gather[k]:
+            c.wait_recv()
+        tile(1, k)
+        forward(k)
+    relay(1)
+    for side, here, copies, k in forwards:
         @pl.when(here)
         def _():
             for c in copies:
                 c.wait_recv()
-            tile(side)
+            tile(side, k)
+
+    for i in range(2, rounds):
+        relay(i)
 
     pair = (picked[...].T * weight[...]).reshape(groups, neigh, go).sum(axis=1)
     for h in range(nhi):
@@ -254,14 +300,11 @@
     type_out[...] = type_row
     type_in[me] = type_row
 
-    def spread(d, carry):
-        p = lax.rem(me + d, total)
-        remote(
-            type_out, type_in.at[me], ty_send.at[0], ty_recv.at[0], {"col": p // nlev, "lev": lax.rem(p, nlev)}
+    visit(
+        lambda c, l: remote(
+            type_out, type_in.at[me], ty_send.at[0], ty_recv.at[0], {"col": c, "lev": l}
         ).start()
-        return carry
-
-    lax.fori_loop(1, total, spread, 0)
+    )
 
     for c in pair_sends:
         c.wait_recv()
@@ -276,16 +319,22 @@
     everyone.wait_recv()
     total_ref[...] = jnp.sum(type_in[...], axis=0)
 
-    for c in scatter + anom_sends + meta_sends + gather + pair_sends:
+    for c in sum(scatter + gather, []) + anom_sends + meta_sends + pair_sends:
         c.wait_send()
-    pl.when(has_left)(to_left.wait_send)
-    pl.when(has_right)(to_right.wait_send)
-    for side, here, copies in forwards:
+    for to_left, to_right in halo:
+        pl.when(has_left)(to_left.wait_send)
+        pl.when(has_right)(to_right.wait_send)
+    for side, here, copies, k in forwards:
         @pl.when(here)
         def _():
             for c in copies:
                 c.wait_send()
     everyone.wait_send()
+
+
+def hand_over(impact_in, total_in, impact_ref, total_ref):
+    impact_ref[...] = impact_in[...]
+    total_ref[...] = total_in[:, :total_ref.shape[1]]
 
 
 def shards(state_anom, error_sum, obs_anom, local_weight, neighbours, innovation, obs_type, live):
@@ -302,6 +351,8 @@
     half = nlo * mq
     depth = -(-3 * half // LANES) * LANES
     total = ncol * nlev
+    chunks = 1 if columns % (2 * LANES) == 0 else 1
+    width = columns // chunks
     dma = pltpu.SemaphoreType.DMA
     f32, bf16, i32 = jnp.float32, jnp.bfloat16, jnp.int32
     vm = pltpu.VMEM
@@ -310,17 +361,19 @@
         vm((max(nlev - 1, 1), mq, columns), f32), vm((3, nlo, mq, columns), f32), vm((nlo, mq, handled), bf16),
         vm((handled, depth), bf16), vm((LANES, go), f32), vm((LANES, go), i32), vm((go, LANES), i32),
         vm((nhi, 1, quarter), f32), vm((nhi, 1, quarter), i32), vm((nhi, 1, quarter), i32),
-        vm((depth, columns), bf16), vm((groups, go, columns), f32), vm((go, LANES), f32),
+        vm((depth, width), bf16), vm((groups, go, width), f32), vm((go, LANES), f32),
         vm((nhi, 1, quarter), f32), vm((max(nhi - 1, 1), 1, quarter), f32),
         vm((1, LANES), f32), vm((total, 1, LANES), f32),
-        dma((1,)), dma((nlev,)), dma((2, groups)), dma((nhi,)), dma((3,)),
-        dma((nlev,)), dma((nlev,)), dma((nlo, nhi)), dma((nlo, nhi)), dma((nhi, 3)), dma((nhi, 3)),
-        dma((nlo,)), dma((nlo,)), dma((2,)), dma((2,)), dma((nlo, 2)), dma((nlo, 2)),
+        pltpu.SemaphoreType.REGULAR((max(1, (ncol - 1).bit_length()),)),
+        dma((1,)), dma((chunks,)), dma((2, groups)), dma((nhi,)), dma((3,)),
+        dma((nlev, chunks)), dma((nlev, chunks)), dma((nlo, nhi)), dma((nlo, nhi)), dma((nhi, 3)), dma((nhi, 3)),
+        dma((nlo, chunks)), dma((nlo, chunks)), dma((2, chunks)), dma((2, chunks)),
+        dma((nlo, 3, chunks)), dma((nlo, 3, chunks)),
         dma((nhi,)), dma((nhi,)), dma((1,)), dma((1,)),
     ]
     anywhere = pl.BlockSpec(memory_space=pl.ANY)
     impact, totals = pl.pallas_call(
-        functools.partial(kernel, (ncol, nlev, nlo, nhi, groups)),
+        functools.partial(kernel, (ncol, nlev, nlo, nhi, groups, chunks)),
         out_shape=(jax.ShapeDtypeStruct((1, quarter), f32), jax.ShapeDtypeStruct((1, LANES), f32)),
         in_specs=[anywhere] * 8,
         out_specs=(pl.BlockSpec(memory_space=pltpu.VMEM), pl.BlockSpec(memory_space=pltpu.VMEM)),
@@ -330,7 +383,10 @@
         state_anom, error_sum, obs_anom, local_weight, neighbours,
         innovation.reshape(1, quarter), obs_type.reshape(1, quarter), live.reshape(1, quarter),
     )
-    return impact.reshape(quarter), totals[0, :NTYPE]
+    impact, totals = pl.pallas_call(
+        hand_over, out_shape=(jax.ShapeDtypeStruct((1, quarter), f32), jax.ShapeDtypeStruct((1, NTYPE), f32))
+    )(impact, totals)
+    return impact.reshape(quarter), totals.reshape(NTYPE)
 
 
 def solution(mesh):

time: 31.3 us -> 26.6 us (0.85)
  local copies, waits for them, and re-layouts: 2.39 us -> 0 us
  Pallas kernels: 28.1 us -> 25.8 us
    pallas_call x1 -> x2, Pallas kernels: 28.1 us -> 25.8 us  [the longest x1 24.5 us: shards(): pl.pallas_call(functools.partial(kernel, (ncol, nlev, nlo, nhi, groups, c...]
    unnamed x1 -> x0, local copies, waits for them, and re-layouts: 1.25 us -> none
    squeeze x1 -> x0, local copies, waits for them, and re-layouts: 1.14 us -> none  [shards(): return (impact.reshape(quarter), totals[0, :NTYPE])]
where the time goes in v3:
time: 26.6 us; the launch traced here: 26.4 us
  Pallas kernels  25.8 us (97%)
  between operations  0.64 us (2%)
    pallas_call x1, Pallas kernels, shards(): pl.pallas_call(functools.partial(kernel, (ncol, nlev, nlo, nhi, groups, c...  24.5 us
    pallas_call x1, Pallas kernels, shards(): pl.pallas_call(hand_over, out_shape=(jax.ShapeDtypeStruct((1, quarter), f...  1.26 us

profile of v3, /device:TPU:0, one launch (start us, length us, event | category | flops | bytes accessed | tf_op | source)
XLA Modules:
  0.0 26.4 jit_solution(2588976940657669825)
XLA Ops:
  0.6 24.5 %shard_map.95 = (f32[1,512]{1,0:T(1,128)}, f32[1,128]{1,0:T(1,128)}) custom-call(bf16[12,64,1024]{2,1,0:T(8,128)(2,1)} %state_hbm.1, f32[12,1024]{1,0:T(8,128)} %error_hbm.1, bf16[16,2048]{1,0:T(8,128)(2,1)} %anom_hbm.1, f32[32,2048]{1,0:T(8,128)} %weight_hbm.1, s32[32,2048]{1,0:T(8,128)} %index_hbm.1, f32[1,512]{1,0:T(1,128)} %bitcast.5, s32[1,512]{1,0:T(1,128)} %bitcast.6, ...), custom_call_target="tpu_custom_call" | custom-call | tf_op jit(solution)/shard_map/pallas_call | solution.py:375
  25.1 1.3 %shard_map.96 = (f32[1,512]{1,0:T(1,128)}, f32[1,32]{1,0:T(1,128)}) custom-call(f32[1,512]{1,0:T(1,128)} %get-tuple-element.6.impact_in, f32[1,128]{1,0:T(1,128)} %get-tuple-element.7.total_in), custom_call_target="tpu_custom_call" | custom-call | tf_op jit(solution)/shard_map/pallas_call | solution.py:386
